TPU v7x, 32 devices: a whole 2x2x4 slice. The times are simulated.
32 devices in a mesh: mode: 16 (over z, y, x), real: 2 (over core).
Axes of the slice: x: 2, y: 2, z: 4, core: 2. Of those that a mesh axis runs over, the one named last changes fastest.
Arguments:
- input_field: bfloat16 [2, 2, 256, 16384], P(None, 'real', 'mode'), may hold values from -6 to 6
- kerr_coeff: bfloat16 [16, 64, 64], P('mode'), may hold values from -0.375 to 0.375
- block_list: int32 [16, 4], P('mode'), may hold values from 0 to 31
Outputs:
- density: float32 [512, 2, 256, 256], P('mode', None, 'real')
All inputs are finite; a program needn't handle non-finite values.
Results may differ from a plain program's by a relative error of at most 0.0085.
Values may be sent and summed in bfloat16 or wider, within the bound.
A program may use at most 64 MiB of HBM per device.

v0:
```python
import math
import jax
import jax.numpy as jnp
from jax import lax
from jax.sharding import PartitionSpec as P

MB = 8
FT = 128
NT = 16384
FB = 32
kerr_strength = 0.25


def kerr_terms(field_blocks, coeff_group, block_group):
    mode_l = jnp.take(field_blocks, block_group[:, 1], axis=2).astype(jnp.float32)
    mode_m = jnp.take(field_blocks, block_group[:, 2], axis=2).astype(jnp.float32)
    mode_n = jnp.take(field_blocks, block_group[:, 3], axis=2).astype(jnp.float32)
    realiz = field_blocks.shape[1]
    group_size = block_group.shape[0]
    steps_local = field_blocks.shape[4]
    prod_re = (
        mode_m[0][:, :, :, None, :] * mode_n[0][:, :, None, :, :]
        + mode_m[1][:, :, :, None, :] * mode_n[1][:, :, None, :, :]
    )
    prod_im = (
        mode_m[1][:, :, :, None, :] * mode_n[0][:, :, None, :, :]
        - mode_m[0][:, :, :, None, :] * mode_n[1][:, :, None, :, :]
    )
    pairs = (
        jnp.stack([prod_re, prod_im])
        .reshape(2, realiz, group_size, MB * MB, steps_local)
        .astype(jnp.bfloat16)
    )
    weighted = jnp.einsum(
        "kab,crkbt->crkat", coeff_group, pairs, preferred_element_type=jnp.float32
    )
    weighted = weighted.reshape(2, realiz, group_size, MB, MB, steps_local)
    term_re = jnp.sum(
        weighted[0] * mode_l[0][:, :, None] - weighted[1] * mode_l[1][:, :, None], axis=3
    )
    term_im = jnp.sum(
        weighted[0] * mode_l[1][:, :, None] + weighted[1] * mode_l[0][:, :, None], axis=3
    )
    one_hot = (
        block_group[:, 0][:, None] == jnp.arange(field_blocks.shape[2], dtype=jnp.int32)[None, :]
    ).astype(jnp.float32)
    return jnp.einsum(
        "kg,crkpt->crgpt", one_hot, jnp.stack([term_re, term_im]), precision=lax.Precision.HIGHEST
    )


def phase_table(extent, modulus):
    index_a = jnp.arange(extent, dtype=jnp.int32)[:, None]
    index_b = jnp.arange(extent, dtype=jnp.int32)[None, :]
    angle = 2.0 * math.pi / modulus * (index_a * index_b % modulus).astype(jnp.float32)
    return (jnp.cos(angle), -jnp.sin(angle))


def first_pass(table, data):
    table_high = table.astype(jnp.bfloat16)
    table_low = (table - table_high.astype(jnp.float32)).astype(jnp.bfloat16)
    upper = jnp.einsum("kn,rmnj->rmkj", table_high, data, preferred_element_type=jnp.float32)
    return upper + jnp.einsum("kn,rmnj->rmkj", table_low, data, preferred_element_type=jnp.float32)


def second_pass(table, data):
    return jnp.einsum("jn,rmkn->rmjk", table, data, precision=lax.Precision.HIGH)


def transform(by_mode):
    realiz = by_mode.shape[1]
    local_modes = by_mode.shape[2]
    signal = by_mode.reshape(2, realiz, local_modes, FT, FT)
    four_re, four_im = phase_table(FT, FT)
    twist_re, twist_im = phase_table(FT, NT)
    half_re = first_pass(four_re, signal[0]) - first_pass(four_im, signal[1])
    half_im = first_pass(four_re, signal[1]) + first_pass(four_im, signal[0])
    turned_re = half_re * twist_re - half_im * twist_im
    turned_im = half_re * twist_im + half_im * twist_re
    out_re = (second_pass(four_re, turned_re) - second_pass(four_im, turned_im)) / FT
    out_im = (second_pass(four_re, turned_im) + second_pass(four_im, turned_re)) / FT
    return jnp.stack([out_re, out_im]).astype(jnp.bfloat16)


def gram_parts(rows_part, cols_part):
    quarters = jnp.einsum(
        "crpbf,drqbf->bcdpq", rows_part, cols_part, preferred_element_type=jnp.float32
    )
    return jnp.stack(
        [quarters[:, 0, 0] + quarters[:, 1, 1], quarters[:, 1, 0] - quarters[:, 0, 1]], axis=1
    )


def shards(input_field, kerr_coeff, block_list):
    timed = lax.all_to_all(input_field, "mode", split_axis=3, concat_axis=2, tiled=True)
    realiz = timed.shape[1]
    width = timed.shape[2]
    steps_local = timed.shape[3]
    field_blocks = timed.reshape(2, realiz, width // MB, MB, steps_local)
    initial = jnp.zeros(field_blocks.shape, jnp.float32)
    running = initial
    coeff_piece = lax.all_gather(kerr_coeff, "mode", axis=0, tiled=True)
    block_piece = lax.all_gather(block_list, "mode", axis=0, tiled=True)
    block_count = block_piece.shape[0]
    coeff_groups = coeff_piece.reshape(
        block_count // 8, 8, coeff_piece.shape[1], coeff_piece.shape[2]
    )
    block_groups = block_piece.reshape(block_count // 8, 8, 4)

    def one_group(carried, groups):
        return (carried + kerr_terms(field_blocks, groups[0], groups[1]), None)

    running, unused = lax.scan(one_group, running, (coeff_groups, block_groups))
    kerr_sum = running
    kerr_sum = kerr_sum.reshape(2, realiz, width, steps_local)
    base = timed.astype(jnp.float32)
    stepped = jnp.stack(
        [base[0] - kerr_strength * kerr_sum[1], base[1] + kerr_strength * kerr_sum[0]]
    ).astype(jnp.bfloat16)
    by_mode = lax.all_to_all(stepped, "mode", split_axis=2, concat_axis=3, tiled=True)
    spectrum = transform(by_mode)
    banded = lax.all_to_all(spectrum, "mode", split_axis=3, concat_axis=2, tiled=True)
    bands_dev = banded.shape[3] * FT // FB
    spec_bands = banded.reshape(2, realiz, width, bands_dev, FB)
    scale = 1.0 / (FB * realiz * lax.axis_size("real"))
    row_count = width // lax.axis_size("real")
    row_first = lax.axis_index("real") * row_count
    shard_piece = lax.all_gather(spec_bands, "real", axis=1, tiled=True)
    own_part = lax.dynamic_slice_in_dim(shard_piece, row_first, row_count, 2)
    return gram_parts(own_part, shard_piece) * scale


def solution(mesh):
    return jax.shard_map(
        shards,
        mesh=mesh,
        in_specs=(P(None, "real", "mode", None), P("mode", None, None), P("mode", None)),
        out_specs=P("mode", None, "real", None),
        check_vma=False,
    )
```

profile of v0, /device:TPU:0, one launch (start us, length us, event | category | flops | bytes accessed | tf_op | source)
XLA Modules:
  0.0 297.2 jit_solution(920240638021889750)
XLA Ops:
  6.5 15.9 %copy.145 = bf16[2,1,16,16384]{2,0,1,3:T(2,128)(2,1)} copy(bf16[2,1,16,16384]{3,2,1,0:T(8,128)(2,1)} %param.7) | data formatting | bytes 2097152 | tf_op args[0]
  22.5 11.2 %reshape.574 = bf16[16,2,16384]{2,1,0:T(2,128)(2,1)} reshape(bf16[16384,1,2,16]{3,2,1,0:T(2,128)(2,1)} %bitcast.267) | data formatting | bytes 2097152
  33.7 8.5 %all-to-all-start = ((bf16[16,2,16384]{2,1,0:T(2,128)(2,1)}), bf16[16,2,16384]{2,1,0:T(2,128)(2,1)S(1)}, u32[]{:S(2)}, u32[]{:S(2)}) async-start(bf16[16,2,16384]{2,1,0:T(2,128)(2,1)} %reshape.574), calls=%async_computation | async-start | bytes 2097152 | tf_op jit(solution)/shard_map/all_to_all | solution.py:95
  42.2 50.9 %all-gather = s32[16,1,4]{2,1,0:T(1,128)S(1)} all-gather(s32[1,1,4]{2,1,0:T(1,128)S(1)} %bitcast.278), channel_id=1, replica_groups=mesh['mode'=16,'real'=2] {'mode'}, dimensions={0}, use_global_device_ids=true | all-gather | bytes 272 | tf_op jit(solution)/shard_map/all_gather | solution.py:103
  93.2 38.7 %all_gather.10 = bf16[16,64,64]{2,1,0:T(8,128)(2,1)S(1)} all-gather(bf16[1,64,64]{2,1,0:T(8,128)(2,1)S(1)} %copy-done.4), channel_id=1, replica_groups=mesh['mode'=16,'real'=2] {'mode'}, dimensions={0}, use_global_device_ids=true | all-gather | bytes 139264 | tf_op jit(solution)/shard_map/all_gather | solution.py:102
  131.8 7.4 %reshape.575 = bf16[16384,1,2,16]{3,2,1,0:T(2,128)(2,1)} reshape(bf16[16,2,16384]{2,1,0:T(2,128)(2,1)S(1)} %all-to-all-done) | data formatting | bytes 2097152
  139.2 17.7 %copy.200 = bf16[2,1,16,16,1024]{4,2,3,0,1:T(8,128)(2,1)S(1)} copy(bf16[2,1,16,16,1024]{2,0,4,3,1:T(2,128)(2,1)} %bitcast.265) | data formatting | bytes 2097152 | tf_op jit(solution)/shard_map/all_to_all | solution.py:95
  156.9 12.7 %copy.197 = bf16[2,1,16,16,1024]{4,3,2,0,1:T(8,128)(2,1)} copy(bf16[2,1,16,16,1024]{2,0,4,3,1:T(2,128)(2,1)} %bitcast.266) | data formatting | bytes 2097152 | tf_op jit(solution)/shard_map/all_to_all | solution.py:95
  169.6 23.4 %while.11 = (s32[]{:T(128)}, f32[2,1,32,8,1024]{4,2,3,0,1:T(8,128)S(1)}, s32[2,8,4]{1,2,0:T(4,128)S(1)}, bf16[2,1,32,8,1024]{4,3,2,1,0:T(8,128)(2,1)S(1)}, bf16[...) while((s32[]{:T(128)}, f32[2,1,32,8,1024]{4,2,3,0,1:T(8,128)S(1)}, ...), condition=%wide.region_3.5_spmd.clone, body=%wide.region_0.4_spmd.clone.sunk | while | flops 198970768 | bytes 36058028 | solution.py:113
  169.7 0.9 copy-done
  170.6 1.8 gather_fusion.2
  172.4 1.8 gather_fusion.1
  174.2 1.8 gather_fusion
  176.4 0.6 fusion.157
  177.0 0.7 convolution_bitcast_fusion.3
  177.7 1.5 subtract_reduce_fusion.2
  179.6 1.7 bitcast_add_fusion.2
  181.4 0.9 copy-done
  182.3 1.8 gather_fusion.2
  184.1 1.8 gather_fusion.1
  185.9 1.8 gather_fusion
  188.1 0.6 fusion.157
  188.8 0.7 convolution_bitcast_fusion.3
  189.5 1.5 subtract_reduce_fusion.2
  191.4 1.7 bitcast_add_fusion.2
  193.1 1.2 copy.152
  194.8 0.6 copy.147
  195.4 0.6 copy.153
  196.7 2.0 copy.155
  198.7 3.7 %all-to-all-start.1 = ((bf16[2,1,256,1024]{3,0,1,2:T(2,128)(2,1)}), bf16[2,1,256,1024]{3,0,1,2:T(2,128)(2,1)S(1)}, u32[]{:S(2)}, u32[]{:S(2)}) async-start(bf16[2,1,256,1024]{3,0,1,2:T(2,128)(2,1)} %copy.155), calls=%async_computation.1 | async-start | bytes 2097152 | tf_op jit(solution)/shard_map/all_to_all | solution.py:120
  203.3 14.6 %all-to-all-done.1 = bf16[2,1,256,1024]{3,0,1,2:T(2,128)(2,1)S(1)} async-done(((bf16[2,1,256,1024]{3,0,1,2:T(2,128)(2,1)}), bf16[2,1,256,1024]{3,0,1,2:T(2,128)(2,1)S(1)}, u32[]{:S(2)}, u32[]{:S(2)}) %all-to-all-start.1) | async-done | bytes 1048608 | tf_op jit(solution)/shard_map/all_to_all | solution.py:120
  218.2 0.9 fusion.137
  220.7 1.1 copy.157
  221.8 1.3 reshape.509
  226.4 1.2 fusion.39
  227.6 1.2 fusion.43
  228.8 1.2 fusion.30
  229.9 1.2 fusion.31
  231.2 1.0 copy.173
  232.2 21.6 %all_to_all.45 = bf16[2,1,16,128,128]{4,2,1,0,3:T(8,128)(2,1)S(1)} all-to-all(bf16[2,1,16,128,128]{4,2,1,0,3:T(8,128)(2,1)S(1)} %copy.173), channel_id=1, replica_groups=mesh['mode'=16,'real'=2] {'mode'}, dimensions={3} | all-to-all | bytes 2097152 | tf_op jit(solution)/shard_map/all_to_all | solution.py:122
  254.5 3.2 %reshape.513 = bf16[2,1,256,32,32]{4,3,2,0,1:T(8,128)(2,1)} reshape(bf16[2,1,16,16,8,128]{5,4,3,2,0,1:T(8,128)(2,1)S(1)} %copy.175) | data formatting | bytes 2097152 | tf_op jit(solution)/shard_map/reshape | solution.py:124
  257.7 5.2 %copy.176 = bf16[2,1,256,32,32]{2,4,1,0,3:T(8,128)(2,1)} copy(bf16[2,1,256,32,32]{4,3,2,0,1:T(8,128)(2,1)} %reshape.513) | data formatting | bytes 2097152 | tf_op jit(solution)/shard_map/reshape | solution.py:124
  263.0 9.0 %all-gather.3.cloned.1.call-done = bf16[2,2,256,32,32]{2,4,1,0,3:T(8,128)(2,1)} async-done(((bf16[2,1,256,32,32]{2,4,1,0,3:T(8,128)(2,1)}), bf16[2,2,256,32,32]{2,4,1,0,3:T(8,128)(2,1)}) %all-gather.3.cloned.1.call-update) | async-done | bytes 2097168 | tf_op jit(solution)/shard_map/all_gather | solution.py:128
  272.0 4.2 %convolution_bitcast_fusion.1 = f32[32,2,2,128,256]{3,4,1,2,0:T(8,128)S(1)} fusion(bf16[2,2,256,32,32]{2,4,1,0,3:T(8,128)(2,1)} %all-gather.3.cloned.1.call-done, s32[]{:T(128)S(6)} %select_n.66), kind=kOutput, calls=%fused_computation.52 | convolution fusion | flops 536870912 | bytes 19922948 | tf_op jit(solution)/shard_map/crpbf,drqbf->bcdpq/dot_general | solution.py:86
  276.2 0.6 fusion.18
  276.9 0.6 fusion.20
  277.5 3.9 %maximum_multiply_fusion = f32[32,2,128,256]{2,3,0,1:T(8,128)} fusion(f32[32,1,128,256]{2,3,0,1:T(8,128)S(1)} %fusion.18, f32[32,1,128,256]{2,3,0,1:T(8,128)S(1)} %fusion.20), kind=kLoop, calls=%fused_computation.53 | loop fusion | flops 4194304 | bytes 16777216 | tf_op jit(solution)/shard_map/mul | solution.py:130
  281.4 8.9 %copy.179 = f32[32,2,128,256]{3,2,1,0:T(8,128)} copy(f32[32,2,128,256]{2,3,0,1:T(8,128)} %maximum_multiply_fusion) | data formatting | bytes 16777216 | tf_op jit(solution)/shard_map/mul | solution.py:130
  (67 shorter events, 9.4 us)
Async XLA Ops:
  33.7 8.5 %copy-start.5 = (s32[1,4]{1,0:T(1,128)S(1)}, s32[1,4]{1,0:T(1,128)}, u32[]{:S(2)}) copy-start(s32[1,4]{1,0:T(1,128)} %param.9) | copy-start | bytes 52
  33.7 59.5 %copy-start.4 = (bf16[1,64,64]{2,1,0:T(8,128)(2,1)S(1)}, bf16[1,64,64]{2,1,0:T(8,128)(2,1)}, u32[]{:S(2)}) copy-start(bf16[1,64,64]{2,1,0:T(8,128)(2,1)} %param.8) | copy-start | bytes 24580
  33.7 98.1 %all-to-all-start = ((bf16[16,2,16384]{2,1,0:T(2,128)(2,1)}), bf16[16,2,16384]{2,1,0:T(2,128)(2,1)S(1)}, u32[]{:S(2)}, u32[]{:S(2)}) async-start(bf16[16,2,16384]{2,1,0:T(2,128)(2,1)} %reshape.574), calls=%async_computation | async-start | bytes 2097152 | tf_op jit(solution)/shard_map/all_to_all | solution.py:95
  169.6 1.0 copy-start
  179.6 1.7 copy-start.1
  181.4 1.0 copy-start
  191.3 1.7 copy-start.1
  193.1 1.2 copy-start.2
  198.7 19.2 %all-to-all-start.1 = ((bf16[2,1,256,1024]{3,0,1,2:T(2,128)(2,1)}), bf16[2,1,256,1024]{3,0,1,2:T(2,128)(2,1)S(1)}, u32[]{:S(2)}, u32[]{:S(2)}) async-start(bf16[2,1,256,1024]{3,0,1,2:T(2,128)(2,1)} %copy.155), calls=%async_computation.1 | async-start | bytes 2097152 | tf_op jit(solution)/shard_map/all_to_all | solution.py:120
  202.4 69.6 %all-gather.3.cloned.1.call-start = ((), (), s32[]{:S(2)}) async-start(), calls=%async_computation.3 | async-start | bytes 3145728 | tf_op jit(solution)/shard_map/all_gather | solution.py:128
  219.6 1.1 copy-start.3
Sparse Core Ops, SparseCore 0:
  263.1 8.8 all-gather.2
where the time goes:
time: 300 us; the launch traced here: 297 us
  blocking collectives  111 us (37%)
  local copies, waits for them, and re-layouts  106 us (35%)
  waiting for transfers between devices  23.6 us (8%)
  matrix products  18.1 us (6%)
  between operations  13.7 us (5%)
  starting transfers between devices  12.3 us (4%)
  other arithmetic  11.5 us (4%)
    all_gather x1, blocking collectives, shards(): block_piece = lax.all_gather(block_list, 'mode', axis=0, tiled=True)  50.9 us
    all_gather x1, blocking collectives, shards(): coeff_piece = lax.all_gather(kerr_coeff, 'mode', axis=0, tiled=True)  38.7 us
    unnamed x12, local copies, waits for them, and re-layouts  34.7 us
    all_to_all x2, local copies, waits for them, and re-layouts, shards(): lax.all_to_all(input_field, 'mode', split_axis=3, concat_axis=2, tiled=True)  30.4 us
    all_to_all x1, blocking collectives, shards(): lax.all_to_all(spectrum, 'mode', split_axis=3, concat_axis=2, tiled=True)  21.6 us
    all_to_all x1, waiting for transfers between devices, shards(): lax.all_to_all(stepped, 'mode', split_axis=2, concat_axis=3, tiled=True)  14.6 us
    all_gather x1, waiting for transfers between devices, shards(): shard_piece = lax.all_gather(spec_bands, 'real', axis=1, tiled=True)  9 us
    mul x1, local copies, waits for them, and re-layouts, shards(): return gram_parts(own_part, shard_piece) * scale  8.94 us
  transfers between devices with their start and end apart: 3, of which 2 were waited for; matrix products, arithmetic and copies ran while one was open for 0% of the time, Pallas kernels for 0%

commit v1 on v0

--- a/solution.py
+++ b/solution.py
@@ -9,6 +9,22 @@
 NT = 16384
 FB = 32
 kerr_strength = 0.25
+
+
+def gather_around(x, axis, dim):
+    ways, here, hop = (lax.axis_size(axis), lax.axis_index(axis), x.shape[dim])
+    lengths = [n * ways if d == dim else n for d, n in enumerate(x.shape)]
+    full = lax.dynamic_update_slice_in_dim(jnp.zeros(lengths, x.dtype), x, here * hop, axis=dim)
+    going_up = going_down = x
+    for far in range(1, ways // 2 + 1):
+        going_up = lax.ppermute(going_up, axis, [(d, (d + 1) % ways) for d in range(ways)])
+        full = lax.dynamic_update_slice_in_dim(full, going_up, (here - far) % ways * hop, axis=dim)
+        if 2 * far < ways:
+            going_down = lax.ppermute(going_down, axis, [(d, (d - 1) % ways) for d in range(ways)])
+            full = lax.dynamic_update_slice_in_dim(
+                full, going_down, (here + far) % ways * hop, axis=dim
+            )
+    return full
 
 
 def kerr_terms(field_blocks, coeff_group, block_group):
@@ -99,7 +115,7 @@
     field_blocks = timed.reshape(2, realiz, width // MB, MB, steps_local)
     initial = jnp.zeros(field_blocks.shape, jnp.float32)
     running = initial
-    coeff_piece = lax.all_gather(kerr_coeff, "mode", axis=0, tiled=True)
+    coeff_piece = gather_around(kerr_coeff, "mode", 0)
     block_piece = lax.all_gather(block_list, "mode", axis=0, tiled=True)
     block_count = block_piece.shape[0]
     coeff_groups = coeff_piece.reshape(

time: 300 us -> 315 us (1.050)
  blocking collectives: 111 us -> 67.1 us
  starting transfers between devices: 12.3 us -> 48.9 us
  waiting for transfers between devices: 23.6 us -> 45.6 us
    all_gather x1 -> x0, blocking collectives: 38.7 us -> none  [shards(): coeff_piece = lax.all_gather(kerr_coeff, 'mode', axis=0, tiled=True)]
    ppermute x0 -> x15, starting transfers between devices: none -> 36.5 us  [the longest x7 36.2 us: gather_around(): lax.ppermute(going_down, axis, [(d, (d - 1) % ways) for d in range(ways)])]
    ppermute x0 -> x15, waiting for transfers between devices: none -> 22 us  [the longest x8 14.6 us: gather_around(): lax.ppermute(going_up, axis, [(d, (d + 1) % ways) for d in range(ways)])]
    all_gather x1, blocking collectives: 50.9 us -> 45.5 us  [shards(): block_piece = lax.all_gather(block_list, 'mode', axis=0, tiled=True)]
  transfers between devices with their start and end apart: 3 -> 18, of which waited for: 2 -> 9; matrix products, arithmetic and copies ran while one was open for 0% -> 0% of each run, Pallas kernels for 0% -> 0%
where the time goes in v1:
time: 315 us; the launch traced here: 312 us
  local copies, waits for them, and re-layouts  107 us (34%)
  blocking collectives  67.1 us (21%)
  starting transfers between devices  48.9 us (16%)
  waiting for transfers between devices  45.6 us (14%)
  matrix products  18.1 us (6%)
  between operations  13.9 us (4%)
  other arithmetic  11.6 us (4%)
    all_gather x1, blocking collectives, shards(): block_piece = lax.all_gather(block_list, 'mode', axis=0, tiled=True)  45.5 us
    ppermute x7, starting transfers between devices, gather_around(): lax.ppermute(going_down, axis, [(d, (d - 1) % ways) for d in range(ways)])  36.2 us
    unnamed x12, local copies, waits for them, and re-layouts  34.7 us
    all_to_all x2, local copies, waits for them, and re-layouts, shards(): lax.all_to_all(input_field, 'mode', split_axis=3, concat_axis=2, tiled=True)  30.4 us
    all_to_all x1, blocking collectives, shards(): lax.all_to_all(spectrum, 'mode', split_axis=3, concat_axis=2, tiled=True)  21.6 us
    ppermute x8, waiting for transfers between devices, gather_around(): lax.ppermute(going_up, axis, [(d, (d + 1) % ways) for d in range(ways)])  14.6 us
    all_to_all x1, waiting for transfers between devices, shards(): lax.all_to_all(stepped, 'mode', split_axis=2, concat_axis=3, tiled=True)  14.6 us
    all_gather x1, waiting for transfers between devices, shards(): shard_piece = lax.all_gather(spec_bands, 'real', axis=1, tiled=True)  9 us
  transfers between devices with their start and end apart: 18, of which 9 were waited for; matrix products, arithmetic and copies ran while one was open for 0% of the time, Pallas kernels for 0%

profile of v1, /device:TPU:0, one launch (start us, length us, event | category | flops | bytes accessed | tf_op | source)
XLA Modules:
  0.0 312.1 jit_solution(2706726568243350774)
XLA Ops:
  6.5 15.9 %copy.145 = bf16[2,1,16,16384]{2,0,1,3:T(2,128)(2,1)} copy(bf16[2,1,16,16384]{3,2,1,0:T(8,128)(2,1)} %param.7) | data formatting | bytes 2097152 | tf_op args[0]
  22.5 11.2 %reshape.574 = bf16[16,2,16384]{2,1,0:T(2,128)(2,1)} reshape(bf16[16384,1,2,16]{3,2,1,0:T(2,128)(2,1)} %bitcast.267) | data formatting | bytes 2097152
  33.7 8.5 %all-to-all-start = ((bf16[16,2,16384]{2,1,0:T(2,128)(2,1)}), bf16[16,2,16384]{2,1,0:T(2,128)(2,1)S(1)}, u32[]{:S(2)}, u32[]{:S(2)}) async-start(bf16[16,2,16384]{2,1,0:T(2,128)(2,1)} %reshape.574), calls=%async_computation | async-start | bytes 2097152 | tf_op jit(solution)/shard_map/all_to_all | solution.py:111
  42.2 5.6 %collective-permute-start.1 = (bf16[1,64,64]{2,1,0:T(8,128)(2,1)S(1)}, bf16[1,64,64]{2,1,0:T(8,128)(2,1)S(1)}, u32[]{:S(2)}, u32[]{:S(2)}) collective-permute-start(bf16[1,64,64]{2,1,0:T(8,128)(2,1)S(1)} %copy-done.4), channel_id=1, source_target_pairs={{0,30},{2,0},{4,2},{6,4},{8,6},{10,8},{12,10},{14,12},{16,14},{18,... | collective-permute-start | bytes 24584 | tf_op jit(solution)/shard_map/ppermute | solution.py:23
  48.0 45.5 %all-gather = s32[16,1,4]{2,1,0:T(1,128)S(1)} all-gather(s32[1,1,4]{2,1,0:T(1,128)S(1)} %bitcast.278), channel_id=1, replica_groups=mesh['mode'=16,'real'=2] {'mode'}, dimensions={0}, use_global_device_ids=true | all-gather | bytes 272 | tf_op jit(solution)/shard_map/all_gather | solution.py:119
  93.6 1.7 collective-permute-start.3
  95.7 1.7 collective-permute-done.3
  97.4 5.3 %collective-permute-start.5 = (bf16[1,64,64]{2,1,0:T(8,128)(2,1)S(1)}, bf16[1,64,64]{2,1,0:T(8,128)(2,1)S(1)}, u32[]{:S(2)}, u32[]{:S(2)}) collective-permute-start(bf16[1,64,64]{2,1,0:T(8,128)(2,1)S(1)} %collective-permute-done.3), channel_id=1, source_target_pairs={{0,30},{2,0},{4,2},{6,4},{8,6},{10,8},{12,10},{14,12},{16,14},{18,... | collective-permute-start | bytes 24584 | tf_op jit(solution)/shard_map/ppermute | solution.py:23
  102.7 1.4 collective-permute-done.5
  104.1 5.9 %collective-permute-start.7 = (bf16[1,64,64]{2,1,0:T(8,128)(2,1)S(1)}, bf16[1,64,64]{2,1,0:T(8,128)(2,1)S(1)}, u32[]{:S(2)}, u32[]{:S(2)}) collective-permute-start(bf16[1,64,64]{2,1,0:T(8,128)(2,1)S(1)} %collective-permute-done.5), channel_id=1, source_target_pairs={{0,30},{2,0},{4,2},{6,4},{8,6},{10,8},{12,10},{14,12},{16,14},{18,... | collective-permute-start | bytes 24584 | tf_op jit(solution)/shard_map/ppermute | solution.py:23
  110.1 1.4 collective-permute-done.7
  111.5 5.9 %collective-permute-start.9 = (bf16[1,64,64]{2,1,0:T(8,128)(2,1)S(1)}, bf16[1,64,64]{2,1,0:T(8,128)(2,1)S(1)}, u32[]{:S(2)}, u32[]{:S(2)}) collective-permute-start(bf16[1,64,64]{2,1,0:T(8,128)(2,1)S(1)} %collective-permute-done.7), channel_id=1, source_target_pairs={{0,30},{2,0},{4,2},{6,4},{8,6},{10,8},{12,10},{14,12},{16,14},{18,... | collective-permute-start | bytes 24584 | tf_op jit(solution)/shard_map/ppermute | solution.py:23
  117.4 1.4 collective-permute-done.9
  118.8 5.9 %collective-permute-start.11 = (bf16[1,64,64]{2,1,0:T(8,128)(2,1)S(1)}, bf16[1,64,64]{2,1,0:T(8,128)(2,1)S(1)}, u32[]{:S(2)}, u32[]{:S(2)}) collective-permute-start(bf16[1,64,64]{2,1,0:T(8,128)(2,1)S(1)} %collective-permute-done.9), channel_id=1, source_target_pairs={{0,30},{2,0},{4,2},{6,4},{8,6},{10,8},{12,10},{14,12},{16,14},{18,... | collective-permute-start | bytes 24584 | tf_op jit(solution)/shard_map/ppermute | solution.py:23
  124.7 1.4 collective-permute-done.11
  126.1 5.9 %collective-permute-start.13 = (bf16[1,64,64]{2,1,0:T(8,128)(2,1)S(1)}, bf16[1,64,64]{2,1,0:T(8,128)(2,1)S(1)}, u32[]{:S(2)}, u32[]{:S(2)}) collective-permute-start(bf16[1,64,64]{2,1,0:T(8,128)(2,1)S(1)} %collective-permute-done.11), channel_id=1, source_target_pairs={{0,30},{2,0},{4,2},{6,4},{8,6},{10,8},{12,10},{14,12},{16,14},{18,... | collective-permute-start | bytes 24584 | tf_op jit(solution)/shard_map/ppermute | solution.py:23
  132.1 7.3 %collective-permute-done.12 = bf16[1,64,64]{2,1,0:T(8,128)(2,1)S(1)} collective-permute-done((bf16[1,64,64]{2,1,0:T(8,128)(2,1)S(1)}, bf16[1,64,64]{2,1,0:T(8,128)(2,1)S(1)}, u32[]{:S(2)}, u32[]{:S(2)}) %collective-permute-start.12) | collective-permute-done | bytes 8224 | tf_op jit(solution)/shard_map/ppermute | solution.py:20
  139.4 7.3 %collective-permute-done.14 = bf16[1,64,64]{2,1,0:T(8,128)(2,1)S(1)} collective-permute-done((bf16[1,64,64]{2,1,0:T(8,128)(2,1)S(1)}, bf16[1,64,64]{2,1,0:T(8,128)(2,1)S(1)}, u32[]{:S(2)}, u32[]{:S(2)}) %collective-permute-start.14) | collective-permute-done | bytes 8224 | tf_op jit(solution)/shard_map/ppermute | solution.py:20
  146.7 7.4 %reshape.575 = bf16[16384,1,2,16]{3,2,1,0:T(2,128)(2,1)} reshape(bf16[16,2,16384]{2,1,0:T(2,128)(2,1)S(1)} %all-to-all-done) | data formatting | bytes 2097152
  154.1 17.7 %copy.200 = bf16[2,1,16,16,1024]{4,2,3,0,1:T(8,128)(2,1)S(1)} copy(bf16[2,1,16,16,1024]{2,0,4,3,1:T(2,128)(2,1)} %bitcast.265) | data formatting | bytes 2097152 | tf_op jit(solution)/shard_map/all_to_all | solution.py:111
  171.8 12.7 %copy.197 = bf16[2,1,16,16,1024]{4,3,2,0,1:T(8,128)(2,1)} copy(bf16[2,1,16,16,1024]{2,0,4,3,1:T(2,128)(2,1)} %bitcast.266) | data formatting | bytes 2097152 | tf_op jit(solution)/shard_map/all_to_all | solution.py:111
  184.5 23.4 %while.11 = (s32[]{:T(128)}, f32[2,1,32,8,1024]{4,2,3,0,1:T(8,128)S(1)}, s32[2,8,4]{1,2,0:T(4,128)S(1)}, bf16[2,1,32,8,1024]{4,3,2,1,0:T(8,128)(2,1)S(1)}, bf16[...) while((s32[]{:T(128)}, f32[2,1,32,8,1024]{4,2,3,0,1:T(8,128)S(1)}, ...), condition=%wide.region_3.5_spmd.clone, body=%wide.region_0.4_spmd.clone.sunk | while | flops 198970768 | bytes 36058028 | solution.py:129
  185.5 1.8 gather_fusion.2
  187.2 1.8 gather_fusion.1
  189.0 1.8 gather_fusion
  192.6 1.5 subtract_reduce_fusion.2
  194.5 1.7 bitcast_add_fusion.2
  197.2 1.8 gather_fusion.2
  199.0 1.8 gather_fusion.1
  200.8 1.8 gather_fusion
  204.3 1.5 subtract_reduce_fusion.2
  206.2 1.7 bitcast_add_fusion.2
  207.9 1.2 copy.152
  211.5 2.0 copy.155
  213.6 3.7 %all-to-all-start.1 = ((bf16[2,1,256,1024]{3,0,1,2:T(2,128)(2,1)}), bf16[2,1,256,1024]{3,0,1,2:T(2,128)(2,1)S(1)}, u32[]{:S(2)}, u32[]{:S(2)}) async-start(bf16[2,1,256,1024]{3,0,1,2:T(2,128)(2,1)} %copy.155), calls=%async_computation.1 | async-start | bytes 2097152 | tf_op jit(solution)/shard_map/all_to_all | solution.py:136
  218.2 14.6 %all-to-all-done.1 = bf16[2,1,256,1024]{3,0,1,2:T(2,128)(2,1)S(1)} async-done(((bf16[2,1,256,1024]{3,0,1,2:T(2,128)(2,1)}), bf16[2,1,256,1024]{3,0,1,2:T(2,128)(2,1)S(1)}, u32[]{:S(2)}, u32[]{:S(2)}) %all-to-all-start.1) | async-done | bytes 1048608 | tf_op jit(solution)/shard_map/all_to_all | solution.py:136
  236.7 1.3 reshape.509
  241.2 1.2 fusion.39
  242.4 1.2 fusion.43
  243.6 1.2 fusion.30
  244.8 1.2 fusion.31
  247.1 21.6 %all_to_all.45 = bf16[2,1,16,128,128]{4,2,1,0,3:T(8,128)(2,1)S(1)} all-to-all(bf16[2,1,16,128,128]{4,2,1,0,3:T(8,128)(2,1)S(1)} %copy.173), channel_id=1, replica_groups=mesh['mode'=16,'real'=2] {'mode'}, dimensions={3} | all-to-all | bytes 2097152 | tf_op jit(solution)/shard_map/all_to_all | solution.py:138
  269.3 3.2 %reshape.513 = bf16[2,1,256,32,32]{4,3,2,0,1:T(8,128)(2,1)} reshape(bf16[2,1,16,16,8,128]{5,4,3,2,0,1:T(8,128)(2,1)S(1)} %copy.175) | data formatting | bytes 2097152 | tf_op jit(solution)/shard_map/reshape | solution.py:140
  272.5 5.2 %copy.176 = bf16[2,1,256,32,32]{2,4,1,0,3:T(8,128)(2,1)} copy(bf16[2,1,256,32,32]{4,3,2,0,1:T(8,128)(2,1)} %reshape.513) | data formatting | bytes 2097152 | tf_op jit(solution)/shard_map/reshape | solution.py:140
  277.8 9.0 %all-gather.3.cloned.1.call-done = bf16[2,2,256,32,32]{2,4,1,0,3:T(8,128)(2,1)} async-done(((bf16[2,1,256,32,32]{2,4,1,0,3:T(8,128)(2,1)}), bf16[2,2,256,32,32]{2,4,1,0,3:T(8,128)(2,1)}) %all-gather.3.cloned.1.call-update) | async-done | bytes 2097168 | tf_op jit(solution)/shard_map/all_gather | solution.py:144
  286.8 4.2 %convolution_bitcast_fusion.1 = f32[32,2,2,128,256]{3,4,1,2,0:T(8,128)S(1)} fusion(bf16[2,2,256,32,32]{2,4,1,0,3:T(8,128)(2,1)} %all-gather.3.cloned.1.call-done, s32[]{:T(128)S(6)} %select_n.207), kind=kOutput, calls=%fused_computation.52 | convolution fusion | flops 536870912 | bytes 19922948 | tf_op jit(solution)/shard_map/crpbf,drqbf->bcdpq/dot_general | solution.py:102
  292.4 3.9 %maximum_multiply_fusion = f32[32,2,128,256]{2,3,0,1:T(8,128)} fusion(f32[32,1,128,256]{2,3,0,1:T(8,128)S(1)} %fusion.18, f32[32,1,128,256]{2,3,0,1:T(8,128)S(1)} %fusion.20), kind=kLoop, calls=%fused_computation.53 | loop fusion | flops 4194304 | bytes 16777216 | tf_op jit(solution)/shard_map/mul | solution.py:146
  296.3 8.9 %copy.179 = f32[32,2,128,256]{3,2,1,0:T(8,128)} copy(f32[32,2,128,256]{2,3,0,1:T(8,128)} %maximum_multiply_fusion) | data formatting | bytes 16777216 | tf_op jit(solution)/shard_map/mul | solution.py:146
  (113 shorter events, 20.0 us)
Async XLA Ops:
  33.7 8.5 %copy-start.4 = (bf16[1,64,64]{2,1,0:T(8,128)(2,1)S(1)}, bf16[1,64,64]{2,1,0:T(8,128)(2,1)}, u32[]{:S(2)}) copy-start(bf16[1,64,64]{2,1,0:T(8,128)(2,1)} %param.8) | copy-start | bytes 24580
  33.7 14.3 %copy-start.5 = (s32[1,4]{1,0:T(1,128)S(1)}, s32[1,4]{1,0:T(1,128)}, u32[]{:S(2)}) copy-start(s32[1,4]{1,0:T(1,128)} %param.9) | copy-start | bytes 52
  33.7 113.0 %all-to-all-start = ((bf16[16,2,16384]{2,1,0:T(2,128)(2,1)}), bf16[16,2,16384]{2,1,0:T(2,128)(2,1)S(1)}, u32[]{:S(2)}, u32[]{:S(2)}) async-start(bf16[16,2,16384]{2,1,0:T(2,128)(2,1)} %reshape.574), calls=%async_computation | async-start | bytes 2097152 | tf_op jit(solution)/shard_map/all_to_all | solution.py:111
  42.2 51.4 %collective-permute-start.1 = (bf16[1,64,64]{2,1,0:T(8,128)(2,1)S(1)}, bf16[1,64,64]{2,1,0:T(8,128)(2,1)S(1)}, u32[]{:S(2)}, u32[]{:S(2)}) collective-permute-start(bf16[1,64,64]{2,1,0:T(8,128)(2,1)S(1)} %copy-done.4), channel_id=1, source_target_pairs={{0,30},{2,0},{4,2},{6,4},{8,6},{10,8},{12,10},{14,12},{16,14},{18,... | collective-permute-start | bytes 24584 | tf_op jit(solution)/shard_map/ppermute | solution.py:23
  47.8 47.6 %collective-permute-start = (bf16[1,64,64]{2,1,0:T(8,128)(2,1)S(1)}, bf16[1,64,64]{2,1,0:T(8,128)(2,1)S(1)}, u32[]{:S(2)}, u32[]{:S(2)}) collective-permute-start(bf16[1,64,64]{2,1,0:T(8,128)(2,1)S(1)} %copy-done.4), channel_id=1, source_target_pairs={{0,2},{2,4},{4,6},{6,8},{8,10},{10,12},{12,14},{14,16},{16,18},{18... | collective-permute-start | bytes 24584 | tf_op jit(solution)/shard_map/ppermute | solution.py:20
  93.6 3.7 %collective-permute-start.3 = (bf16[1,64,64]{2,1,0:T(8,128)(2,1)S(1)}, bf16[1,64,64]{2,1,0:T(8,128)(2,1)S(1)}, u32[]{:S(2)}, u32[]{:S(2)}) collective-permute-start(bf16[1,64,64]{2,1,0:T(8,128)(2,1)S(1)} %collective-permute-done.1), channel_id=1, source_target_pairs={{0,30},{2,0},{4,2},{6,4},{8,6},{10,8},{12,10},{14,12},{16,14},{18,... | collective-permute-start | bytes 24584 | tf_op jit(solution)/shard_map/ppermute | solution.py:23
  95.4 7.3 %collective-permute-start.2 = (bf16[1,64,64]{2,1,0:T(8,128)(2,1)S(1)}, bf16[1,64,64]{2,1,0:T(8,128)(2,1)S(1)}, u32[]{:S(2)}, u32[]{:S(2)}) collective-permute-start(bf16[1,64,64]{2,1,0:T(8,128)(2,1)S(1)} %collective-permute-done), channel_id=1, source_target_pairs={{0,2},{2,4},{4,6},{6,8},{8,10},{10,12},{12,14},{14,16},{16,18},{18... | collective-permute-start | bytes 24584 | tf_op jit(solution)/shard_map/ppermute | solution.py:20
  97.4 6.8 %collective-permute-start.5 = (bf16[1,64,64]{2,1,0:T(8,128)(2,1)S(1)}, bf16[1,64,64]{2,1,0:T(8,128)(2,1)S(1)}, u32[]{:S(2)}, u32[]{:S(2)}) collective-permute-start(bf16[1,64,64]{2,1,0:T(8,128)(2,1)S(1)} %collective-permute-done.3), channel_id=1, source_target_pairs={{0,30},{2,0},{4,2},{6,4},{8,6},{10,8},{12,10},{14,12},{16,14},{18,... | collective-permute-start | bytes 24584 | tf_op jit(solution)/shard_map/ppermute | solution.py:23
  102.7 7.3 %collective-permute-start.4 = (bf16[1,64,64]{2,1,0:T(8,128)(2,1)S(1)}, bf16[1,64,64]{2,1,0:T(8,128)(2,1)S(1)}, u32[]{:S(2)}, u32[]{:S(2)}) collective-permute-start(bf16[1,64,64]{2,1,0:T(8,128)(2,1)S(1)} %collective-permute-done.2), channel_id=1, source_target_pairs={{0,2},{2,4},{4,6},{6,8},{8,10},{10,12},{12,14},{14,16},{16,18},{18... | collective-permute-start | bytes 24584 | tf_op jit(solution)/shard_map/ppermute | solution.py:20
  104.1 7.3 %collective-permute-start.7 = (bf16[1,64,64]{2,1,0:T(8,128)(2,1)S(1)}, bf16[1,64,64]{2,1,0:T(8,128)(2,1)S(1)}, u32[]{:S(2)}, u32[]{:S(2)}) collective-permute-start(bf16[1,64,64]{2,1,0:T(8,128)(2,1)S(1)} %collective-permute-done.5), channel_id=1, source_target_pairs={{0,30},{2,0},{4,2},{6,4},{8,6},{10,8},{12,10},{14,12},{16,14},{18,... | collective-permute-start | bytes 24584 | tf_op jit(solution)/shard_map/ppermute | solution.py:23
  110.0 7.3 %collective-permute-start.6 = (bf16[1,64,64]{2,1,0:T(8,128)(2,1)S(1)}, bf16[1,64,64]{2,1,0:T(8,128)(2,1)S(1)}, u32[]{:S(2)}, u32[]{:S(2)}) collective-permute-start(bf16[1,64,64]{2,1,0:T(8,128)(2,1)S(1)} %collective-permute-done.4), channel_id=1, source_target_pairs={{0,2},{2,4},{4,6},{6,8},{8,10},{10,12},{12,14},{14,16},{16,18},{18... | collective-permute-start | bytes 24584 | tf_op jit(solution)/shard_map/ppermute | solution.py:20
  111.5 7.3 %collective-permute-start.9 = (bf16[1,64,64]{2,1,0:T(8,128)(2,1)S(1)}, bf16[1,64,64]{2,1,0:T(8,128)(2,1)S(1)}, u32[]{:S(2)}, u32[]{:S(2)}) collective-permute-start(bf16[1,64,64]{2,1,0:T(8,128)(2,1)S(1)} %collective-permute-done.7), channel_id=1, source_target_pairs={{0,30},{2,0},{4,2},{6,4},{8,6},{10,8},{12,10},{14,12},{16,14},{18,... | collective-permute-start | bytes 24584 | tf_op jit(solution)/shard_map/ppermute | solution.py:23
  117.4 7.3 %collective-permute-start.8 = (bf16[1,64,64]{2,1,0:T(8,128)(2,1)S(1)}, bf16[1,64,64]{2,1,0:T(8,128)(2,1)S(1)}, u32[]{:S(2)}, u32[]{:S(2)}) collective-permute-start(bf16[1,64,64]{2,1,0:T(8,128)(2,1)S(1)} %collective-permute-done.6), channel_id=1, source_target_pairs={{0,2},{2,4},{4,6},{6,8},{8,10},{10,12},{12,14},{14,16},{16,18},{18... | collective-permute-start | bytes 24584 | tf_op jit(solution)/shard_map/ppermute | solution.py:20
  118.8 7.3 %collective-permute-start.11 = (bf16[1,64,64]{2,1,0:T(8,128)(2,1)S(1)}, bf16[1,64,64]{2,1,0:T(8,128)(2,1)S(1)}, u32[]{:S(2)}, u32[]{:S(2)}) collective-permute-start(bf16[1,64,64]{2,1,0:T(8,128)(2,1)S(1)} %collective-permute-done.9), channel_id=1, source_target_pairs={{0,30},{2,0},{4,2},{6,4},{8,6},{10,8},{12,10},{14,12},{16,14},{18,... | collective-permute-start | bytes 24584 | tf_op jit(solution)/shard_map/ppermute | solution.py:23
  124.7 7.3 %collective-permute-start.10 = (bf16[1,64,64]{2,1,0:T(8,128)(2,1)S(1)}, bf16[1,64,64]{2,1,0:T(8,128)(2,1)S(1)}, u32[]{:S(2)}, u32[]{:S(2)}) collective-permute-start(bf16[1,64,64]{2,1,0:T(8,128)(2,1)S(1)} %collective-permute-done.8), channel_id=1, source_target_pairs={{0,2},{2,4},{4,6},{6,8},{8,10},{10,12},{12,14},{14,16},{16,18},{18... | collective-permute-start | bytes 24584 | tf_op jit(solution)/shard_map/ppermute | solution.py:20
  126.1 13.2 %collective-permute-start.13 = (bf16[1,64,64]{2,1,0:T(8,128)(2,1)S(1)}, bf16[1,64,64]{2,1,0:T(8,128)(2,1)S(1)}, u32[]{:S(2)}, u32[]{:S(2)}) collective-permute-start(bf16[1,64,64]{2,1,0:T(8,128)(2,1)S(1)} %collective-permute-done.11), channel_id=1, source_target_pairs={{0,30},{2,0},{4,2},{6,4},{8,6},{10,8},{12,10},{14,12},{16,14},{18,... | collective-permute-start | bytes 24584 | tf_op jit(solution)/shard_map/ppermute | solution.py:23
  132.0 7.3 %collective-permute-start.12 = (bf16[1,64,64]{2,1,0:T(8,128)(2,1)S(1)}, bf16[1,64,64]{2,1,0:T(8,128)(2,1)S(1)}, u32[]{:S(2)}, u32[]{:S(2)}) collective-permute-start(bf16[1,64,64]{2,1,0:T(8,128)(2,1)S(1)} %collective-permute-done.10), channel_id=1, source_target_pairs={{0,2},{2,4},{4,6},{6,8},{8,10},{10,12},{12,14},{14,16},{16,18},{18... | collective-permute-start | bytes 24584 | tf_op jit(solution)/shard_map/ppermute | solution.py:20
  139.4 7.3 %collective-permute-start.14 = (bf16[1,64,64]{2,1,0:T(8,128)(2,1)S(1)}, bf16[1,64,64]{2,1,0:T(8,128)(2,1)S(1)}, u32[]{:S(2)}, u32[]{:S(2)}) collective-permute-start(bf16[1,64,64]{2,1,0:T(8,128)(2,1)S(1)} %collective-permute-done.12), channel_id=1, source_target_pairs={{0,2},{2,4},{4,6},{6,8},{8,10},{10,12},{12,14},{14,16},{16,18},{18... | collective-permute-start | bytes 24584 | tf_op jit(solution)/shard_map/ppermute | solution.py:20
  184.5 1.0 copy-start
  194.5 1.7 copy-start.1
  196.2 1.0 copy-start
  206.2 1.7 copy-start.1
  207.9 1.2 copy-start.2
  213.6 19.2 %all-to-all-start.1 = ((bf16[2,1,256,1024]{3,0,1,2:T(2,128)(2,1)}), bf16[2,1,256,1024]{3,0,1,2:T(2,128)(2,1)S(1)}, u32[]{:S(2)}, u32[]{:S(2)}) async-start(bf16[2,1,256,1024]{3,0,1,2:T(2,128)(2,1)} %copy.155), calls=%async_computation.1 | async-start | bytes 2097152 | tf_op jit(solution)/shard_map/all_to_all | solution.py:136
  217.2 69.6 %all-gather.3.cloned.1.call-start = ((), (), s32[]{:S(2)}) async-start(), calls=%async_computation.3 | async-start | bytes 3145728 | tf_op jit(solution)/shard_map/all_gather | solution.py:144
  234.5 1.1 copy-start.3
Sparse Core Ops, SparseCore 0:
  277.9 8.8 all-gather.2
